TPU v7x, 32 devices: a whole 2x2x4 slice. The times are simulated.
32 devices in a mesh: rows: 8 (over z, y), cols: 4 (over x, core).
Axes of the slice: x: 2, y: 2, z: 4, core: 2. Of those that a mesh axis runs over, the one named last changes fastest.
Arguments:
- depth: float32 [128, 16384], P('rows', 'cols'), may hold values from 0.08 to 6.3, as said below
- hit_mask: int32 [128, 16384], P('rows', 'cols'), may hold values 0 or 1
- hit_count: int32 [128, 16384], P('rows', 'cols'), may hold values from 1 to 8
- grad_h: float32 [128, 16384], P('rows', 'cols'), may hold values from -6 to 6
- grad_v: float32 [128, 16384], P('rows', 'cols'), may hold values from -6 to 6
Outputs:
- solution_field: float32 [128, 16384], P('rows', 'cols')
- residual: float32 [128, 16384], P('rows', 'cols')
Inputs may be any that keep to these rules, and one draw needn't show every extreme that they name: `depth`: positive depths.
All inputs are finite; a program needn't handle non-finite values. No bound on the sum of `hit_mask` on one device may be relied on, other than what follows from the above.
Results may differ from a plain program's by a relative error of at most 0.0003.
Values sent between devices are 32-bit elements; how exact they have to be, the bound alone decides.
A program may use at most 64 MiB of HBM per device.

v0:
```python
import jax
import jax.numpy as jnp
from jax import lax
from jax.sharding import PartitionSpec as P

ITERS = 12


prior_weight = 0.1
smooth_weight = 2.0


def passed_along(value, axis, steps):
    count = lax.axis_size(axis)
    first, last = (max(0, -steps), min(count, count - steps))
    return lax.ppermute(value, axis, [(source, source + steps) for source in range(first, last)])


def extended(cells, sides, width):
    for axis, dim in sides:
        count = lax.axis_size(axis)
        ends = count - 1
        head = lax.slice_in_dim(cells, 0, width, axis=dim)
        tail = lax.slice_in_dim(cells, cells.shape[dim] - width, cells.shape[dim], axis=dim)
        cells = jnp.concatenate(
            [
                lax.ppermute(tail, axis, [(i, (i + 1) % count) for i in range(ends)]),
                cells,
                lax.ppermute(head, axis, [((i + 1) % count, i) for i in range(ends)]),
            ],
            axis=dim,
        )
    return cells


def stencil(padded, field, coefficients):
    center, east, west, south, north = coefficients
    beside = (
        east * padded[1:-1, 2:]
        + west * padded[1:-1, :-2]
        + south * padded[2:, 1:-1]
        + north * padded[:-2, 1:-1]
    )
    return center * field - smooth_weight * beside


def paired(residual, watched):
    return lax.psum((jnp.sum(residual * residual), jnp.sum(watched * residual)), ("rows", "cols"))


def on_device(depth, hit_mask, hit_count, grad_h, grad_v):
    rows_here, cols_here = depth.shape
    total_rows = rows_here * lax.axis_size("rows")
    total_cols = cols_here * lax.axis_size("cols")
    global_row = lax.axis_index("rows") * rows_here + lax.broadcasted_iota(
        jnp.int32, depth.shape, 0
    )
    global_col = lax.axis_index("cols") * cols_here + lax.broadcasted_iota(
        jnp.int32, depth.shape, 1
    )
    east = jnp.where(global_col + 1 < total_cols, jnp.exp(-0.5 * grad_h * grad_h), 0.0)
    south = jnp.where(global_row + 1 < total_rows, jnp.exp(-0.5 * grad_v * grad_v), 0.0)
    confidence = (hit_mask * hit_count).astype(jnp.float32) + prior_weight
    right_side = confidence * depth
    zeros = jnp.zeros_like(right_side)
    unity = jnp.ones((), jnp.float32)
    east_before = passed_along(east[:, -1:], "cols", 1)
    south_before = passed_along(south[-1:, :], "rows", 1)
    west = jnp.concatenate([east_before, east[:, :-1]], axis=1)
    north = jnp.concatenate([south_before, south[:-1, :]], axis=0)
    center = confidence + smooth_weight * (east + west + south + north)
    coefficients = (center, east, west, south, north)
    every = 1

    def apply(field):
        padded = extended(field, (("rows", 0), ("cols", 1)), 1)
        return stencil(padded, field, coefficients)

    def widen(fields):
        return tuple(fields)

    def run_groups(count, start, renew, advance, state):

        def group(number, state):
            state = renew(state)
            state = advance(start + number * every + 0, state)
            return state

        return lax.fori_loop(0, count, group, state)

    def relayed_iteration(index, state):
        solution_field, residual, watched, folded_sum, shadow, direction, gamma_old, alpha_old = (
            state
        )
        gamma, delta = paired(residual, watched)
        folded = apply(watched)
        beta = jnp.where(index == 0, 0.0, gamma / gamma_old)
        alpha = gamma / (delta - beta * gamma / alpha_old)
        folded_sum = folded + beta * folded_sum
        shadow = watched + beta * shadow
        direction = residual + beta * direction
        solution_field = solution_field + alpha * direction
        residual = residual - alpha * shadow
        watched = watched - alpha * folded_sum
        return (solution_field, residual, watched, folded_sum, shadow, direction, gamma, alpha)

    def renew_relayed(state):
        solution_field, residual, watched, folded_sum, shadow, direction, gamma_old, alpha_old = (
            state
        )
        residual, watched, folded_sum, shadow = widen((residual, watched, folded_sum, shadow))
        return (
            solution_field,
            residual,
            watched,
            folded_sum,
            shadow,
            direction,
            gamma_old,
            alpha_old,
        )

    wide_right = widen((right_side,))[0]
    watched = apply(wide_right)
    wide_zeros = jnp.zeros_like(wide_right)
    start_state = (zeros, wide_right, watched, wide_zeros, wide_zeros, zeros, unity, unity)
    state = relayed_iteration(0, start_state)
    solution_field, residual, watched, folded_sum, shadow, direction, gamma_old, alpha_old = (
        run_groups((ITERS - 2) // every, 1, renew_relayed, relayed_iteration, state)
    )
    gamma, delta = paired(residual, watched)
    beta = gamma / gamma_old
    alpha = gamma / (delta - beta * gamma / alpha_old)
    shadow = watched + beta * shadow
    direction = residual + beta * direction
    solution_field = solution_field + alpha * direction
    residual = residual - alpha * shadow
    return (solution_field, residual)


def solution(mesh):
    placed = (
        P("rows", "cols"),
        P("rows", "cols"),
        P("rows", "cols"),
        P("rows", "cols"),
        P("rows", "cols"),
    )
    return jax.shard_map(
        on_device,
        mesh=mesh,
        in_specs=placed,
        out_specs=(P("rows", "cols"), P("rows", "cols")),
        check_vma=False,
    )
```

profile of v0, /device:TPU:0, one launch (start us, length us, event | category | flops | bytes accessed | tf_op | source)
XLA Modules:
  0.0 718.8 jit_solution(9165617761868551327)
XLA Ops:
  1.8 4.9 collective-permute-start.5
  11.5 4.5 collective-permute-start.6
  24.1 46.0 %all-reduce.2 = (f32[]{:T(128)}, f32[]{:T(128)}) all-reduce(f32[]{:T(128)} %get-tuple-element.323, f32[]{:T(128)} %get-tuple-element.322), channel_id=1, replica_groups=mesh['rows'=8,'cols'=4] {'rows','cols'}, use_global_device_ids=true, to_apply=%region_1.2 | all-reduce | flops 2 | bytes 16 | tf_op jit(solution)/shard_map/psum | solution.py:48
  73.3 5.0 collective-permute-start.10
  86.1 588.0 %while.27 = (s32[]{:T(128)}, f32[16,4096]{1,0:T(8,128)S(1)}, f32[16,4096]{1,0:T(8,128)S(1)}, f32[16,4096]{1,0:T(8,128)S(1)}, f32[16,4096]{1,0:T(8,128)S(1)}, /*i...) while((s32[]{:T(128)}, f32[16,4096]{1,0:T(8,128)S(1)}, ...), condition=%wide.region_9.10_spmd, body=%wide.region_4.9_spmd.sunk | while | flops 2228305 | bytes 5768495 | solution.py:89
  86.1 4.8 collective-permute-start
  92.9 45.2 %all-reduce.4 = (f32[]{:T(128)}, f32[]{:T(128)}) all-reduce(f32[]{:T(128)} %get-tuple-element.547, f32[]{:T(128)} %get-tuple-element.548), channel_id=1, replica_groups=mesh['rows'=8,'cols'=4] {'rows','cols'}, use_global_device_ids=true, to_apply=%region_6.6 | all-reduce | flops 2 | bytes 16 | tf_op jit(solution)/shard_map/while/body/eval_jaxpr/psum | solution.py:48
  143.6 4.3 collective-permute-done.3
  149.0 4.1 collective-permute-start
  155.0 42.3 %all-reduce.4 = (f32[]{:T(128)}, f32[]{:T(128)}) all-reduce(f32[]{:T(128)} %get-tuple-element.547, f32[]{:T(128)} %get-tuple-element.548), channel_id=1, replica_groups=mesh['rows'=8,'cols'=4] {'rows','cols'}, use_global_device_ids=true, to_apply=%region_6.6 | all-reduce | flops 2 | bytes 16 | tf_op jit(solution)/shard_map/while/body/eval_jaxpr/psum | solution.py:48
  202.8 4.3 collective-permute-done.3
  212.9 41.8 %all-reduce.4 = (f32[]{:T(128)}, f32[]{:T(128)}) all-reduce(f32[]{:T(128)} %get-tuple-element.547, f32[]{:T(128)} %get-tuple-element.548), channel_id=1, replica_groups=mesh['rows'=8,'cols'=4] {'rows','cols'}, use_global_device_ids=true, to_apply=%region_6.6 | all-reduce | flops 2 | bytes 16 | tf_op jit(solution)/shard_map/while/body/eval_jaxpr/psum | solution.py:48
  260.2 4.3 collective-permute-done.3
  265.6 3.9 collective-permute-start
  271.4 42.4 %all-reduce.4 = (f32[]{:T(128)}, f32[]{:T(128)}) all-reduce(f32[]{:T(128)} %get-tuple-element.547, f32[]{:T(128)} %get-tuple-element.548), channel_id=1, replica_groups=mesh['rows'=8,'cols'=4] {'rows','cols'}, use_global_device_ids=true, to_apply=%region_6.6 | all-reduce | flops 2 | bytes 16 | tf_op jit(solution)/shard_map/while/body/eval_jaxpr/psum | solution.py:48
  319.3 4.3 collective-permute-done.3
  329.4 41.7 %all-reduce.4 = (f32[]{:T(128)}, f32[]{:T(128)}) all-reduce(f32[]{:T(128)} %get-tuple-element.547, f32[]{:T(128)} %get-tuple-element.548), channel_id=1, replica_groups=mesh['rows'=8,'cols'=4] {'rows','cols'}, use_global_device_ids=true, to_apply=%region_6.6 | all-reduce | flops 2 | bytes 16 | tf_op jit(solution)/shard_map/while/body/eval_jaxpr/psum | solution.py:48
  376.6 4.3 collective-permute-done.3
  382.0 4.0 collective-permute-start
  387.9 42.4 %all-reduce.4 = (f32[]{:T(128)}, f32[]{:T(128)}) all-reduce(f32[]{:T(128)} %get-tuple-element.547, f32[]{:T(128)} %get-tuple-element.548), channel_id=1, replica_groups=mesh['rows'=8,'cols'=4] {'rows','cols'}, use_global_device_ids=true, to_apply=%region_6.6 | all-reduce | flops 2 | bytes 16 | tf_op jit(solution)/shard_map/while/body/eval_jaxpr/psum | solution.py:48
  435.7 4.3 collective-permute-done.3
  446.0 41.6 %all-reduce.4 = (f32[]{:T(128)}, f32[]{:T(128)}) all-reduce(f32[]{:T(128)} %get-tuple-element.547, f32[]{:T(128)} %get-tuple-element.548), channel_id=1, replica_groups=mesh['rows'=8,'cols'=4] {'rows','cols'}, use_global_device_ids=true, to_apply=%region_6.6 | all-reduce | flops 2 | bytes 16 | tf_op jit(solution)/shard_map/while/body/eval_jaxpr/psum | solution.py:48
  493.1 4.3 collective-permute-done.3
  498.5 4.0 collective-permute-start
  504.4 42.4 %all-reduce.4 = (f32[]{:T(128)}, f32[]{:T(128)}) all-reduce(f32[]{:T(128)} %get-tuple-element.547, f32[]{:T(128)} %get-tuple-element.548), channel_id=1, replica_groups=mesh['rows'=8,'cols'=4] {'rows','cols'}, use_global_device_ids=true, to_apply=%region_6.6 | all-reduce | flops 2 | bytes 16 | tf_op jit(solution)/shard_map/while/body/eval_jaxpr/psum | solution.py:48
  552.2 4.3 collective-permute-done.3
  562.5 41.6 %all-reduce.4 = (f32[]{:T(128)}, f32[]{:T(128)}) all-reduce(f32[]{:T(128)} %get-tuple-element.547, f32[]{:T(128)} %get-tuple-element.548), channel_id=1, replica_groups=mesh['rows'=8,'cols'=4] {'rows','cols'}, use_global_device_ids=true, to_apply=%region_6.6 | all-reduce | flops 2 | bytes 16 | tf_op jit(solution)/shard_map/while/body/eval_jaxpr/psum | solution.py:48
  609.6 4.3 collective-permute-done.3
  615.0 4.0 collective-permute-start
  620.8 42.4 %all-reduce.4 = (f32[]{:T(128)}, f32[]{:T(128)}) all-reduce(f32[]{:T(128)} %get-tuple-element.547, f32[]{:T(128)} %get-tuple-element.548), channel_id=1, replica_groups=mesh['rows'=8,'cols'=4] {'rows','cols'}, use_global_device_ids=true, to_apply=%region_6.6 | all-reduce | flops 2 | bytes 16 | tf_op jit(solution)/shard_map/while/body/eval_jaxpr/psum | solution.py:48
  668.7 4.3 collective-permute-done.3
  674.7 40.0 %all-reduce.1 = (f32[]{:T(128)}, f32[]{:T(128)}) all-reduce(f32[]{:T(128)} %get-tuple-element.319, f32[]{:T(128)} %get-tuple-element.318), channel_id=1, replica_groups=mesh['rows'=8,'cols'=4] {'rows','cols'}, use_global_device_ids=true, to_apply=%region_11.12 | all-reduce | flops 2 | bytes 16 | tf_op jit(solution)/shard_map/psum | solution.py:48
  (159 shorter events, 89.0 us)
Async XLA Ops:
  1.8 7.4 %collective-permute-start.5 = (f32[1,4096]{1,0:T(1,128)S(1)}, f32[1,4096]{1,0:T(1,128)S(1)}, u32[]{:S(2)}, u32[]{:S(2)}) collective-permute-start(f32[1,4096]{1,0:T(1,128)S(1)} %slice.150), channel_id=1, source_target_pairs={{0,4},{4,8},{8,12},{12,16},{16,20},{20,24},{24,28},{1,5},{5,9},{9,... | collective-permute-start | bytes 49160 | tf_op jit(solution)/shard_map/ppermute | solution.py:16
  10.2 5.9 collective-permute-start.7
  11.5 6.0 collective-permute-start.6
  72.0 6.3 collective-permute-start.11
  73.3 6.4 collective-permute-start.10
  86.1 54.7 %collective-permute-start = (f32[1,4096]{1,0:T(1,128)S(1)}, f32[1,4096]{1,0:T(1,128)S(1)}, u32[]{:S(2)}, u32[]{:S(2)}) collective-permute-start(f32[1,4096]{1,0:T(1,128)S(1)} %get-tuple-element.503), channel_id=1, source_target_pairs={{0,4},{4,8},{8,12},{12,16},{16,20},{20,24},{24,28},{1,5},{5,9},{9,... | collective-permute-start | bytes 49160 | tf_op jit(solution)/shard_map/while/body/eval_jaxpr/ppermute | solution.py:27
  91.0 49.9 %collective-permute-start.1 = (f32[1,4096]{1,0:T(1,128)S(1)}, f32[1,4096]{1,0:T(1,128)S(1)}, u32[]{:S(2)}, u32[]{:S(2)}) collective-permute-start(f32[1,4096]{1,0:T(1,128)S(1)} %get-tuple-element.504), channel_id=1, source_target_pairs={{4,0},{8,4},{12,8},{16,12},{20,16},{24,20},{28,24},{5,1},{9,5},{13... | collective-permute-start | bytes 49160 | tf_op jit(solution)/shard_map/while/body/eval_jaxpr/ppermute | solution.py:29
  142.3 5.6 collective-permute-start.3
  149.0 51.1 %collective-permute-start = (f32[1,4096]{1,0:T(1,128)S(1)}, f32[1,4096]{1,0:T(1,128)S(1)}, u32[]{:S(2)}, u32[]{:S(2)}) collective-permute-start(f32[1,4096]{1,0:T(1,128)S(1)} %get-tuple-element.503), channel_id=1, source_target_pairs={{0,4},{4,8},{8,12},{12,16},{16,20},{20,24},{24,28},{1,5},{5,9},{9,... | collective-permute-start | bytes 49160 | tf_op jit(solution)/shard_map/while/body/eval_jaxpr/ppermute | solution.py:27
  153.0 47.1 %collective-permute-start.1 = (f32[1,4096]{1,0:T(1,128)S(1)}, f32[1,4096]{1,0:T(1,128)S(1)}, u32[]{:S(2)}, u32[]{:S(2)}) collective-permute-start(f32[1,4096]{1,0:T(1,128)S(1)} %get-tuple-element.504), channel_id=1, source_target_pairs={{4,0},{8,4},{12,8},{16,12},{20,16},{24,20},{28,24},{5,1},{9,5},{13... | collective-permute-start | bytes 49160 | tf_op jit(solution)/shard_map/while/body/eval_jaxpr/ppermute | solution.py:29
  201.5 5.6 collective-permute-start.3
  208.2 49.4 %collective-permute-start = (f32[1,4096]{1,0:T(1,128)S(1)}, f32[1,4096]{1,0:T(1,128)S(1)}, u32[]{:S(2)}, u32[]{:S(2)}) collective-permute-start(f32[1,4096]{1,0:T(1,128)S(1)} %get-tuple-element.503), channel_id=1, source_target_pairs={{0,4},{4,8},{8,12},{12,16},{16,20},{20,24},{24,28},{1,5},{5,9},{9,... | collective-permute-start | bytes 49160 | tf_op jit(solution)/shard_map/while/body/eval_jaxpr/ppermute | solution.py:27
  211.0 46.6 %collective-permute-start.1 = (f32[1,4096]{1,0:T(1,128)S(1)}, f32[1,4096]{1,0:T(1,128)S(1)}, u32[]{:S(2)}, u32[]{:S(2)}) collective-permute-start(f32[1,4096]{1,0:T(1,128)S(1)} %get-tuple-element.504), channel_id=1, source_target_pairs={{4,0},{8,4},{12,8},{16,12},{20,16},{24,20},{28,24},{5,1},{9,5},{13... | collective-permute-start | bytes 49160 | tf_op jit(solution)/shard_map/while/body/eval_jaxpr/ppermute | solution.py:29
  258.9 5.6 collective-permute-start.3
  265.6 51.0 %collective-permute-start = (f32[1,4096]{1,0:T(1,128)S(1)}, f32[1,4096]{1,0:T(1,128)S(1)}, u32[]{:S(2)}, u32[]{:S(2)}) collective-permute-start(f32[1,4096]{1,0:T(1,128)S(1)} %get-tuple-element.503), channel_id=1, source_target_pairs={{0,4},{4,8},{8,12},{12,16},{16,20},{20,24},{24,28},{1,5},{5,9},{9,... | collective-permute-start | bytes 49160 | tf_op jit(solution)/shard_map/while/body/eval_jaxpr/ppermute | solution.py:27
  269.5 47.1 %collective-permute-start.1 = (f32[1,4096]{1,0:T(1,128)S(1)}, f32[1,4096]{1,0:T(1,128)S(1)}, u32[]{:S(2)}, u32[]{:S(2)}) collective-permute-start(f32[1,4096]{1,0:T(1,128)S(1)} %get-tuple-element.504), channel_id=1, source_target_pairs={{4,0},{8,4},{12,8},{16,12},{20,16},{24,20},{28,24},{5,1},{9,5},{13... | collective-permute-start | bytes 49160 | tf_op jit(solution)/shard_map/while/body/eval_jaxpr/ppermute | solution.py:29
  324.6 49.3 %collective-permute-start = (f32[1,4096]{1,0:T(1,128)S(1)}, f32[1,4096]{1,0:T(1,128)S(1)}, u32[]{:S(2)}, u32[]{:S(2)}) collective-permute-start(f32[1,4096]{1,0:T(1,128)S(1)} %get-tuple-element.503), channel_id=1, source_target_pairs={{0,4},{4,8},{8,12},{12,16},{16,20},{20,24},{24,28},{1,5},{5,9},{9,... | collective-permute-start | bytes 49160 | tf_op jit(solution)/shard_map/while/body/eval_jaxpr/ppermute | solution.py:27
  327.5 46.4 %collective-permute-start.1 = (f32[1,4096]{1,0:T(1,128)S(1)}, f32[1,4096]{1,0:T(1,128)S(1)}, u32[]{:S(2)}, u32[]{:S(2)}) collective-permute-start(f32[1,4096]{1,0:T(1,128)S(1)} %get-tuple-element.504), channel_id=1, source_target_pairs={{4,0},{8,4},{12,8},{16,12},{20,16},{24,20},{28,24},{5,1},{9,5},{13... | collective-permute-start | bytes 49160 | tf_op jit(solution)/shard_map/while/body/eval_jaxpr/ppermute | solution.py:29
  375.3 5.6 collective-permute-start.3
  382.0 51.0 %collective-permute-start = (f32[1,4096]{1,0:T(1,128)S(1)}, f32[1,4096]{1,0:T(1,128)S(1)}, u32[]{:S(2)}, u32[]{:S(2)}) collective-permute-start(f32[1,4096]{1,0:T(1,128)S(1)} %get-tuple-element.503), channel_id=1, source_target_pairs={{0,4},{4,8},{8,12},{12,16},{16,20},{20,24},{24,28},{1,5},{5,9},{9,... | collective-permute-start | bytes 49160 | tf_op jit(solution)/shard_map/while/body/eval_jaxpr/ppermute | solution.py:27
  386.0 47.1 %collective-permute-start.1 = (f32[1,4096]{1,0:T(1,128)S(1)}, f32[1,4096]{1,0:T(1,128)S(1)}, u32[]{:S(2)}, u32[]{:S(2)}) collective-permute-start(f32[1,4096]{1,0:T(1,128)S(1)} %get-tuple-element.504), channel_id=1, source_target_pairs={{4,0},{8,4},{12,8},{16,12},{20,16},{24,20},{28,24},{5,1},{9,5},{13... | collective-permute-start | bytes 49160 | tf_op jit(solution)/shard_map/while/body/eval_jaxpr/ppermute | solution.py:29
  434.4 5.6 collective-permute-start.3
  441.1 49.3 %collective-permute-start = (f32[1,4096]{1,0:T(1,128)S(1)}, f32[1,4096]{1,0:T(1,128)S(1)}, u32[]{:S(2)}, u32[]{:S(2)}) collective-permute-start(f32[1,4096]{1,0:T(1,128)S(1)} %get-tuple-element.503), channel_id=1, source_target_pairs={{0,4},{4,8},{8,12},{12,16},{16,20},{20,24},{24,28},{1,5},{5,9},{9,... | collective-permute-start | bytes 49160 | tf_op jit(solution)/shard_map/while/body/eval_jaxpr/ppermute | solution.py:27
  444.1 46.4 %collective-permute-start.1 = (f32[1,4096]{1,0:T(1,128)S(1)}, f32[1,4096]{1,0:T(1,128)S(1)}, u32[]{:S(2)}, u32[]{:S(2)}) collective-permute-start(f32[1,4096]{1,0:T(1,128)S(1)} %get-tuple-element.504), channel_id=1, source_target_pairs={{4,0},{8,4},{12,8},{16,12},{20,16},{24,20},{28,24},{5,1},{9,5},{13... | collective-permute-start | bytes 49160 | tf_op jit(solution)/shard_map/while/body/eval_jaxpr/ppermute | solution.py:29
  491.8 5.6 collective-permute-start.3
  498.5 51.1 %collective-permute-start = (f32[1,4096]{1,0:T(1,128)S(1)}, f32[1,4096]{1,0:T(1,128)S(1)}, u32[]{:S(2)}, u32[]{:S(2)}) collective-permute-start(f32[1,4096]{1,0:T(1,128)S(1)} %get-tuple-element.503), channel_id=1, source_target_pairs={{0,4},{4,8},{8,12},{12,16},{16,20},{20,24},{24,28},{1,5},{5,9},{9,... | collective-permute-start | bytes 49160 | tf_op jit(solution)/shard_map/while/body/eval_jaxpr/ppermute | solution.py:27
  502.4 47.1 %collective-permute-start.1 = (f32[1,4096]{1,0:T(1,128)S(1)}, f32[1,4096]{1,0:T(1,128)S(1)}, u32[]{:S(2)}, u32[]{:S(2)}) collective-permute-start(f32[1,4096]{1,0:T(1,128)S(1)} %get-tuple-element.504), channel_id=1, source_target_pairs={{4,0},{8,4},{12,8},{16,12},{20,16},{24,20},{28,24},{5,1},{9,5},{13... | collective-permute-start | bytes 49160 | tf_op jit(solution)/shard_map/while/body/eval_jaxpr/ppermute | solution.py:29
  550.9 5.6 collective-permute-start.3
  557.6 49.3 %collective-permute-start = (f32[1,4096]{1,0:T(1,128)S(1)}, f32[1,4096]{1,0:T(1,128)S(1)}, u32[]{:S(2)}, u32[]{:S(2)}) collective-permute-start(f32[1,4096]{1,0:T(1,128)S(1)} %get-tuple-element.503), channel_id=1, source_target_pairs={{0,4},{4,8},{8,12},{12,16},{16,20},{20,24},{24,28},{1,5},{5,9},{9,... | collective-permute-start | bytes 49160 | tf_op jit(solution)/shard_map/while/body/eval_jaxpr/ppermute | solution.py:27
  560.6 46.3 %collective-permute-start.1 = (f32[1,4096]{1,0:T(1,128)S(1)}, f32[1,4096]{1,0:T(1,128)S(1)}, u32[]{:S(2)}, u32[]{:S(2)}) collective-permute-start(f32[1,4096]{1,0:T(1,128)S(1)} %get-tuple-element.504), channel_id=1, source_target_pairs={{4,0},{8,4},{12,8},{16,12},{20,16},{24,20},{28,24},{5,1},{9,5},{13... | collective-permute-start | bytes 49160 | tf_op jit(solution)/shard_map/while/body/eval_jaxpr/ppermute | solution.py:29
  615.0 51.1 %collective-permute-start = (f32[1,4096]{1,0:T(1,128)S(1)}, f32[1,4096]{1,0:T(1,128)S(1)}, u32[]{:S(2)}, u32[]{:S(2)}) collective-permute-start(f32[1,4096]{1,0:T(1,128)S(1)} %get-tuple-element.503), channel_id=1, source_target_pairs={{0,4},{4,8},{8,12},{12,16},{16,20},{20,24},{24,28},{1,5},{5,9},{9,... | collective-permute-start | bytes 49160 | tf_op jit(solution)/shard_map/while/body/eval_jaxpr/ppermute | solution.py:27
  618.9 47.1 %collective-permute-start.1 = (f32[1,4096]{1,0:T(1,128)S(1)}, f32[1,4096]{1,0:T(1,128)S(1)}, u32[]{:S(2)}, u32[]{:S(2)}) collective-permute-start(f32[1,4096]{1,0:T(1,128)S(1)} %get-tuple-element.504), channel_id=1, source_target_pairs={{4,0},{8,4},{12,8},{16,12},{20,16},{24,20},{28,24},{5,1},{9,5},{13... | collective-permute-start | bytes 49160 | tf_op jit(solution)/shard_map/while/body/eval_jaxpr/ppermute | solution.py:29
  (23 other events, 82.5 us)
where the time goes:
time: 723 us; the launch traced here: 719 us
  blocking collectives  510 us (71%)
  starting transfers between devices  102 us (14%)
  waiting for transfers between devices  48 us (7%)
  loops' own time  32.2 us (4%)
  other arithmetic  19.1 us (3%)
    psum x12, blocking collectives, paired(): lax.psum((jnp.sum(residual * residual), jnp.sum(watched * residual)), ('r...  510 us
    ppermute x24, starting transfers between devices, extended(): lax.ppermute(tail, axis, [(i, (i + 1) % count) for i in range(ends)])  65 us
    ppermute x24, waiting for transfers between devices, extended(): lax.ppermute(head, axis, [((i + 1) % count, i) for i in range(ends)])  42.8 us
    another operation x1, loops' own time, run_groups(): return lax.fori_loop(0, count, group, state)  32.2 us
    ppermute x24, starting transfers between devices, extended(): lax.ppermute(head, axis, [((i + 1) % count, i) for i in range(ends)])  31 us
  transfers between devices with their start and end apart: 50, of which 15 were waited for; matrix products, arithmetic and copies ran while one was open for 0% of the time, Pallas kernels for 0%

commit v1 on v0

v1 whole, which is shorter than its diff:
```python
import functools

import jax
import jax.numpy as jnp
from jax import lax
from jax.experimental import pallas as pl
from jax.experimental.pallas import tpu as pltpu
from jax.sharding import PartitionSpec as P

ITERS = 12

prior_weight = 0.1
smooth_weight = 2.0
LANES = 128
MESH = pl.DeviceIdType.MESH


def each(start, stop, body):
    if stop - start <= 8:
        for k in range(start, stop):
            body(k)
    else:
        lax.fori_loop(start, stop, lambda k, c: (body(k), c)[1], 0)


def kernel(
    nr, nc,
    depth, hit_mask, hit_count, grad_h, grad_v,
    x, r,
    conf, east, south, w, z, s, p, n,
    e_left, s_above, e_send, s_send,
    left, right, above, below, first_tile, last_tile, top, bottom,
    by_col, by_row,
    coef_send, coef_recv, halo_send, halo_recv, col_send, col_recv, row_send, row_recv,
):
    me_r = lax.axis_index("rows")
    me_c = lax.axis_index("cols")
    rows, cols = depth.shape
    tiles = cols // LANES
    has_above, has_below = me_r > 0, me_r < nr - 1
    has_left, has_right = me_c > 0, me_c < nc - 1

    def row_peer(k):
        return (lax.rem(me_r + k, nr), me_c)

    def col_peer(k):
        return (me_r, lax.rem(me_c + k, nc))

    barrier = pltpu.get_barrier_semaphore()
    each(1, nr, lambda k: pl.semaphore_signal(barrier, inc=1, device_id=row_peer(k), device_id_type=MESH))
    each(1, nc, lambda k: pl.semaphore_signal(barrier, inc=1, device_id=col_peer(k), device_id_type=MESH))

    row_id = lax.broadcasted_iota(jnp.int32, (rows, LANES), 0)
    lane_id = lax.broadcasted_iota(jnp.int32, (rows, LANES), 1)

    def at(j):
        return slice(j * LANES, (j + 1) * LANES)

    for j in range(tiles):
        c = at(j)
        confidence = (hit_mask[:, c] * hit_count[:, c]).astype(jnp.float32) + prior_weight
        h, v = grad_h[:, c], grad_v[:, c]
        e = smooth_weight * jnp.exp(-0.5 * h * h)
        if j == tiles - 1:
            e = jnp.where(jnp.logical_and(lane_id == LANES - 1, jnp.logical_not(has_right)), 0.0, e)
        so = smooth_weight * jnp.exp(-0.5 * v * v)
        so = jnp.where(jnp.logical_and(row_id == rows - 1, jnp.logical_not(has_below)), 0.0, so)
        b = confidence * depth[:, c]
        zero = jnp.zeros((rows, LANES), jnp.float32)
        conf[:, c] = confidence
        east[:, c] = e
        south[:, c] = so
        r[:, c] = b
        x[:, c] = zero
        z[:, c] = zero
        s[:, c] = zero
        p[:, c] = zero
        s_send[:, c] = so[rows - 1 :, :]
        top[:, c] = b[:1, :]
        bottom[:, c] = b[rows - 1 :, :]
        if j == 0:
            first_tile[...] = b
        if j == tiles - 1:
            last_tile[...] = b
            e_send[...] = e

    @pl.when(jnp.logical_not(has_above))
    def _():
        s_above[...] = jnp.zeros_like(s_above)
        above[...] = jnp.zeros_like(above)

    @pl.when(jnp.logical_not(has_below))
    def _():
        below[...] = jnp.zeros_like(below)

    @pl.when(jnp.logical_not(has_left))
    def _():
        e_left[...] = jnp.zeros_like(e_left)
        left[...] = jnp.zeros_like(left)

    @pl.when(jnp.logical_not(has_right))
    def _():
        right[...] = jnp.zeros_like(right)

    pl.semaphore_wait(barrier, nr - 1 + nc - 1)

    up, down = (me_r - 1, me_c), (me_r + 1, me_c)
    lefthand, righthand = (me_r, me_c - 1), (me_r, me_c + 1)

    def remote(src, dst, send, recv, to):
        return pltpu.make_async_remote_copy(
            src_ref=src, dst_ref=dst, send_sem=send, recv_sem=recv, device_id=to, device_id_type=MESH
        )

    def halo_copies(slot):
        return (
            (remote(top, below.at[slot], halo_send.at[0], halo_recv.at[slot, 0], up), has_above, has_below),
            (remote(bottom, above.at[slot], halo_send.at[1], halo_recv.at[slot, 1], down), has_below, has_above),
            (remote(first_tile, right.at[slot], halo_send.at[2], halo_recv.at[slot, 2], lefthand), has_left, has_right),
            (remote(last_tile, left.at[slot], halo_send.at[3], halo_recv.at[slot, 3], righthand), has_right, has_left),
        )

    def coef_copies():
        return (
            (remote(s_send, s_above, coef_send.at[0], coef_recv.at[0], down), has_below, has_above),
            (remote(e_send, e_left, coef_send.at[1], coef_recv.at[1], righthand), has_right, has_left),
        )

    def start(copies):
        for copy, sends, _ in copies:
            pl.when(sends)(copy.start)

    def wait_recv(copies):
        for copy, _, receives in copies:
            pl.when(receives)(copy.wait_recv)

    def wait_send(copies):
        for copy, sends, _ in copies:
            pl.when(sends)(copy.wait_send)

    def stencil(src, slot, emit):
        def to_left(v):
            return pltpu.roll(v, LANES - 1, 1)

        def to_right(v):
            return pltpu.roll(v, 1, 1)

        v = src[:, at(0)]
        moved = to_left(v)
        before = left[slot]
        flow = e_left[...] * (before - jnp.where(lane_id < LANES - 1, to_left(before), moved))
        carried = to_right(flow)
        for j in range(tiles):
            c = at(j)
            following = src[:, at(j + 1)] if j + 1 < tiles else right[slot]
            moved_next = to_left(following)
            flow = east[:, c] * (v - jnp.where(lane_id < LANES - 1, moved, moved_next))
            shifted = to_right(flow)
            from_left = jnp.where(lane_id > 0, shifted, carried)
            lower = jnp.where(row_id < rows - 1, pltpu.roll(v, rows - 1, 0), below[slot, :, c])
            fall = south[:, c] * (v - lower)
            upper = s_above[:, c] * (above[slot, :, c] - v)
            from_above = jnp.where(row_id > 0, pltpu.roll(fall, 1, 0), upper)
            emit(c, v, conf[:, c] * v + ((flow - from_left) + (fall - from_above)))
            v, moved, carried = following, moved_next, shifted

    def folded(acc):
        return jnp.sum(acc, axis=0, keepdims=True)

    first, coefs = halo_copies(0), coef_copies()
    start(first)
    start(coefs)
    wait_recv(first)
    wait_recv(coefs)
    wait_send(first)
    wait_send(coefs)
    acc = [jnp.zeros((rows, LANES), jnp.float32)] * 2

    def keep_edges(c, value):
        top[:, c] = value[:1, :]
        bottom[:, c] = value[rows - 1 :, :]
        if c.start == 0:
            first_tile[...] = value
        if c.stop == cols:
            last_tile[...] = value

    def begin(c, v, image):
        w[:, c] = image
        keep_edges(c, image)
        acc[0] = acc[0] + v * v
        acc[1] = acc[1] + v * image

    stencil(r, 0, begin)

    def reduce_cols(slot, rr, rw):
        by_col[slot, me_c, 0:1, :] = folded(rr)
        by_col[slot, me_c, 1:2, :] = folded(rw)

        def copy(k, source):
            return remote(by_col.at[slot, me_c], by_col.at[slot, me_c], col_send.at[k], col_recv.at[slot, source], col_peer(k))

        each(1, nc, lambda k: copy(k, me_c).start())

        def finish():
            def arrival(k):
                source = lax.rem(me_c + k, nc)
                here = by_col.at[slot, source]
                remote(here, here, col_send.at[k], col_recv.at[slot, source], col_peer(k)).wait_recv()

            each(1, nc, arrival)
            each(1, nc, lambda k: copy(k, me_c).wait_send())
            total = by_col[slot, 0]
            for k in range(1, nc):
                total = total + by_col[slot, k]
            return total

        return finish

    def reduce_rows(slot, part):
        by_row[slot, me_r] = part

        def copy(k):
            return remote(by_row.at[slot, me_r], by_row.at[slot, me_r], row_send.at[k], row_recv.at[slot, me_r], row_peer(k))

        each(1, nr, lambda k: copy(k).start())

        def finish():
            def arrival(k):
                source = lax.rem(me_r + k, nr)
                here = by_row.at[slot, source]
                remote(here, here, row_send.at[k], row_recv.at[slot, source], row_peer(k)).wait_recv()

            each(1, nr, arrival)
            each(1, nr, lambda k: copy(k).wait_send())
            if nr <= 8:
                total = by_row[slot, 0]
                for k in range(1, nr):
                    total = total + by_row[slot, k]
            else:
                total = lax.fori_loop(1, nr, lambda k, t: t + by_row[slot, k], by_row[slot, 0])
            total = jnp.sum(total, axis=1, keepdims=True)
            return total[0:1], total[1:2]

        return finish

    def wide(scalar):
        return jnp.broadcast_to(scalar, (rows, LANES))

    def iteration(i, state, last=False):
        rr, rw, gamma_old, alpha_old = state
        slot = lax.rem(i + 1, 2)
        halos = () if last else halo_copies(slot)
        finish_cols = reduce_cols(slot, rr, rw)
        start(halos)
        finish_rows = reduce_rows(slot, finish_cols())
        wait_recv(halos)

        def keep(c, v, image):
            n[:, c] = image

        if not last:
            stencil(w, slot, keep)
        wait_send(halos)
        gamma, delta = finish_rows()
        beta = gamma / gamma_old
        beta = jnp.where(i == 0, jnp.zeros_like(beta), beta)
        alpha = gamma / (delta - beta * gamma / alpha_old)
        a, b = wide(alpha), wide(beta)
        rr = jnp.zeros((rows, LANES), jnp.float32)
        rw = rr
        for j in range(tiles):
            c = at(j)
            shadow = w[:, c] + b * s[:, c]
            direction = r[:, c] + b * p[:, c]
            x[:, c] = x[:, c] + a * direction
            residual = r[:, c] - a * shadow
            r[:, c] = residual
            if not last:
                images = n[:, c] + b * z[:, c]
                watched = w[:, c] - a * images
                s[:, c] = shadow
                p[:, c] = direction
                z[:, c] = images
                w[:, c] = watched
                keep_edges(c, watched)
                rr = rr + residual * residual
                rw = rw + residual * watched
        return rr, rw, gamma, alpha

    unity = jnp.ones((1, 1), jnp.float32)
    state = lax.fori_loop(0, ITERS - 1, iteration, (acc[0], acc[1], unity, unity))
    iteration(ITERS - 1, state, last=True)


def solution(mesh):
    nr, nc = mesh.shape["rows"], mesh.shape["cols"]

    def on_device(*inputs):
        rows, cols = inputs[0].shape
        block = jax.ShapeDtypeStruct((rows, cols), jnp.float32)

        def held(*shape):
            return pltpu.VMEM(shape, jnp.float32)

        dma = pltpu.SemaphoreType.DMA
        return pl.pallas_call(
            functools.partial(kernel, nr, nc),
            out_shape=(block, block),
            in_specs=[pl.BlockSpec(memory_space=pltpu.VMEM)] * 5,
            out_specs=[pl.BlockSpec(memory_space=pltpu.VMEM)] * 2,
            scratch_shapes=[held(rows, cols)] * 8
            + [held(rows, LANES), held(1, cols), held(rows, LANES), held(1, cols)]
            + [held(2, rows, LANES), held(2, rows, LANES), held(2, 1, cols), held(2, 1, cols)]
            + [held(rows, LANES), held(rows, LANES), held(1, cols), held(1, cols)]
            + [held(2, nc, 2, LANES), held(2, nr, 2, LANES)]
            + [dma((2,)), dma((2,)), dma((4,)), dma((2, 4)), dma((nc,)), dma((2, nc)), dma((nr,)), dma((2, nr))],
            compiler_params=pltpu.CompilerParams(collective_id=0, has_side_effects=True),
        )(*inputs)

    spec = P("rows", "cols")
    return jax.shard_map(
        on_device, mesh=mesh, in_specs=(spec,) * 5, out_specs=(spec, spec), check_vma=False
    )
```

time: 723 us -> 96.4 us (0.13)
  blocking collectives: 510 us -> 0 us
  starting transfers between devices: 102 us -> 0 us
  Pallas kernels: 0 us -> 93.2 us
  waiting for transfers between devices: 48 us -> 0 us
  loops' own time: 32.2 us -> 0 us
  other arithmetic: 19.1 us -> 0 us
    psum x12 -> x0, blocking collectives: 510 us -> none  [paired(): lax.psum((jnp.sum(residual * residual), jnp.sum(watched * residual)), ('r...]
    ppermute x50 -> x0, starting transfers between devices: 102 us -> none  [the longest x24 65 us: extended(): lax.ppermute(tail, axis, [(i, (i + 1) % count) for i in range(ends)])]
    pallas_call x0 -> x1, Pallas kernels: none -> 93.2 us  [on_device(): pl.pallas_call(functools.partial(kernel, nr, nc), out_shape=(block, block...]
    ppermute x50 -> x0, waiting for transfers between devices: 48 us -> none  [the longest x24 42.8 us: extended(): lax.ppermute(head, axis, [((i + 1) % count, i) for i in range(ends)])]
    another operation x1 -> x0, loops' own time: 32.2 us -> none  [run_groups(): return lax.fori_loop(0, count, group, state)]
    reduce_sum x13 -> x0, other arithmetic: 13.3 us -> none  [paired(): jnp.sum(watched * residual)]
  transfers between devices with their start and end apart: 50 -> 0, of which waited for: 15 -> 0; matrix products, arithmetic and copies ran while one was open for 0% -> 0% of each run, Pallas kernels for 0% -> 0%
where the time goes in v1:
time: 96.4 us; the launch traced here: 96.3 us
  Pallas kernels  93.2 us (97%)
  local copies, waits for them, and re-layouts  2.42 us (3%)
    pallas_call x1, Pallas kernels, on_device(): pl.pallas_call(functools.partial(kernel, nr, nc), out_shape=(block, block...  93.2 us
    unnamed x4, local copies, waits for them, and re-layouts  2.42 us

profile of v1, /device:TPU:0, one launch (start us, length us, event | category | flops | bytes accessed | tf_op | source)
XLA Modules:
  0.0 96.3 jit_solution(879809470350409378)
XLA Ops:
  0.6 93.2 %shard_map.68 = (f32[16,4096]{1,0:T(8,128)}, f32[16,4096]{1,0:T(8,128)}) custom-call(f32[16,4096]{1,0:T(8,128)} %depth.1, s32[16,4096]{1,0:T(8,128)} %hit_mask.1, s32[16,4096]{1,0:T(8,128)} %hit_count.1, f32[16,4096]{1,0:T(8,128)} %grad_h.1, f32[16,4096]{1,0:T(8,128)} %grad_v.1), custom_call_target="tpu_custom_call" | custom-call | tf_op jit(solution)/shard_map/pallas_call | solution.py:306
  93.9 0.0 copy-start
  93.9 1.7 %copy.9 = f32[16,4096]{1,0:T(8,128)} copy(f32[16,4096]{1,0:T(8,128)} %get-tuple-element.4) | data formatting | bytes 524288
  95.6 0.0 copy-done
  95.6 0.7 copy.10
Async XLA Ops:
  93.9 1.7 %copy-start = (f32[16,4096]{1,0:T(8,128)S(1)}, f32[16,4096]{1,0:T(8,128)}, u32[]{:S(2)}) copy-start(f32[16,4096]{1,0:T(8,128)} %get-tuple-element.5) | copy-start | bytes 786436

commit v2 on v1

--- a/solution.py
+++ b/solution.py
@@ -12,6 +12,7 @@
 prior_weight = 0.1
 smooth_weight = 2.0
 LANES = 128
+DOTS = 10
 MESH = pl.DeviceIdType.MESH
 
 
@@ -26,8 +27,8 @@
 def kernel(
     nr, nc,
     depth, hit_mask, hit_count, grad_h, grad_v,
-    x, r,
-    conf, east, south, w, z, s, p, n,
+    x, r0,
+    conf, east, south, r1, r2, r3, q0, q1, q2, old2,
     e_left, s_above, e_send, s_send,
     left, right, above, below, first_tile, last_tile, top, bottom,
     by_col, by_row,
@@ -70,11 +71,9 @@
         conf[:, c] = confidence
         east[:, c] = e
         south[:, c] = so
-        r[:, c] = b
-        x[:, c] = zero
-        z[:, c] = zero
-        s[:, c] = zero
-        p[:, c] = zero
+        r0[:, c] = b
+        for held in (x, q0, q1, q2, old2):
+            held[:, c] = zero
         s_send[:, c] = so[rows - 1 :, :]
         top[:, c] = b[:1, :]
         bottom[:, c] = b[rows - 1 :, :]
@@ -167,14 +166,8 @@
     def folded(acc):
         return jnp.sum(acc, axis=0, keepdims=True)
 
-    first, coefs = halo_copies(0), coef_copies()
-    start(first)
-    start(coefs)
-    wait_recv(first)
-    wait_recv(coefs)
-    wait_send(first)
-    wait_send(coefs)
-    acc = [jnp.zeros((rows, LANES), jnp.float32)] * 2
+    def folded(acc):
+        return jnp.sum(acc, axis=0, keepdims=True)
 
     def keep_edges(c, value):
         top[:, c] = value[:1, :]
@@ -184,17 +177,9 @@
         if c.stop == cols:
             last_tile[...] = value
 
-    def begin(c, v, image):
-        w[:, c] = image
-        keep_edges(c, image)
-        acc[0] = acc[0] + v * v
-        acc[1] = acc[1] + v * image
-
-    stencil(r, 0, begin)
-
-    def reduce_cols(slot, rr, rw):
-        by_col[slot, me_c, 0:1, :] = folded(rr)
-        by_col[slot, me_c, 1:2, :] = folded(rw)
+    def reduce_cols(slot, sums):
+        for k in range(DOTS):
+            by_col[slot, me_c, k : k + 1, :] = folded(sums[k])
 
         def copy(k, source):
             return remote(by_col.at[slot, me_c], by_col.at[slot, me_c], col_send.at[k], col_recv.at[slot, source], col_peer(k))
@@ -217,7 +202,9 @@
         return finish
 
     def reduce_rows(slot, part):
-        by_row[slot, me_r] = part
+        part = jnp.broadcast_to(jnp.sum(part, axis=1, keepdims=True), (DOTS, LANES))
+        mine = lax.broadcasted_iota(jnp.int32, (DOTS, LANES), 0) == lax.broadcasted_iota(jnp.int32, (DOTS, LANES), 1)
+        by_row[slot, me_r] = folded(jnp.where(mine, part, 0.0))
 
         def copy(k):
             return remote(by_row.at[slot, me_r], by_row.at[slot, me_r], row_send.at[k], row_recv.at[slot, me_r], row_peer(k))
@@ -238,58 +225,116 @@
                     total = total + by_row[slot, k]
             else:
                 total = lax.fori_loop(1, nr, lambda k, t: t + by_row[slot, k], by_row[slot, 0])
-            total = jnp.sum(total, axis=1, keepdims=True)
-            return total[0:1], total[1:2]
+            return [total[:, k : k + 1] for k in range(DOTS)]
 
         return finish
 
     def wide(scalar):
         return jnp.broadcast_to(scalar, (rows, LANES))
 
-    def iteration(i, state, last=False):
-        rr, rw, gamma_old, alpha_old = state
-        slot = lax.rem(i + 1, 2)
-        halos = () if last else halo_copies(slot)
-        finish_cols = reduce_cols(slot, rr, rw)
+    def added(sums, pairs):
+        return tuple(total + a * b for total, (a, b) in zip(sums, pairs))
+
+    def stencil_into(dst, edges):
+        def emit(c, v, image):
+            dst[:, c] = image
+            if edges:
+                keep_edges(c, image)
+
+        return emit
+
+    def exchange(slot):
+        halos = halo_copies(slot)
         start(halos)
-        finish_rows = reduce_rows(slot, finish_cols())
+        return halos
+
+    def arrive(halos):
         wait_recv(halos)
-
-        def keep(c, v, image):
-            n[:, c] = image
-
+        wait_send(halos)
+
+    first, coefs = exchange(1), coef_copies()
+    start(coefs)
+    arrive(first)
+    arrive(coefs)
+    none = jnp.zeros((rows, LANES), jnp.float32)
+    opening = [(none,) * 3]
+
+    def begin(c, v, image):
+        r1[:, c] = image
+        keep_edges(c, image)
+        opening[0] = added(opening[0], ((v, v), (v, image), (image, image)))
+
+    stencil(r0, 1, begin)
+
+    def block(i, state, last=False):
+        sums, gamma_old, alpha_old = state
+        slot = lax.rem(i, 2)
+        arrive(exchange(0))
+        cross = [(none,)]
+
+        def second(c, v, image):
+            r2[:, c] = image
+            if not last:
+                keep_edges(c, image)
+            cross[0] = added(cross[0], ((v, image),))
+
+        stencil(r1, 0, second)
         if not last:
-            stencil(w, slot, keep)
-        wait_send(halos)
-        gamma, delta = finish_rows()
-        beta = gamma / gamma_old
-        beta = jnp.where(i == 0, jnp.zeros_like(beta), beta)
-        alpha = gamma / (delta - beta * gamma / alpha_old)
-        a, b = wide(alpha), wide(beta)
-        rr = jnp.zeros((rows, LANES), jnp.float32)
-        rw = rr
+            halos = exchange(1)
+        finish_rows = reduce_rows(slot, reduce_cols(slot, sums + cross[0])())
+        if not last:
+            arrive(halos)
+            stencil(r2, 1, stencil_into(r3, False))
+        r0r0, r0r1, r1r1, r0q1, q0q1, r1q1, q1q1, r1q2, q1q2, r1r2 = finish_rows()
+        beta = jnp.where(i == 0, jnp.zeros_like(r0r0), r0r0 / gamma_old)
+        pap = r0r1 + beta * (2.0 * r0q1 + beta * q0q1)
+        r0p1 = r0r1 + beta * r0q1
+        p1p1 = r1r1 + beta * (2.0 * r1q1 + beta * q1q1)
+        r1p1 = r1r1 + beta * r1q1
+        p1p2 = r1r2 + beta * (2.0 * r1q2 + beta * q1q2)
+        alpha = r0r0 / pap
+        gamma = r0r0 - alpha * (2.0 * r0p1 - alpha * p1p1)
+        beta_next = gamma / r0r0
+        m0p1 = r0p1 - alpha * p1p1
+        m0m1 = r0r1 - alpha * (2.0 * r1p1 - alpha * p1p2)
+        alpha_next = gamma / (m0m1 + beta_next * (2.0 * m0p1 + beta_next * pap))
+        b, a, b_, a_ = wide(beta), wide(alpha), wide(beta_next), wide(alpha_next)
+        inverse = wide(1.0 / alpha_old)
+        sums = (none,) * (DOTS - 1)
         for j in range(tiles):
             c = at(j)
-            shadow = w[:, c] + b * s[:, c]
-            direction = r[:, c] + b * p[:, c]
-            x[:, c] = x[:, c] + a * direction
-            residual = r[:, c] - a * shadow
-            r[:, c] = residual
+            v0, v1, v2 = r0[:, c], r1[:, c], r2[:, c]
+            p0 = v0 + b * q0[:, c]
+            p1 = v1 + b * q1[:, c]
+            p2 = v2 + b * q2[:, c]
+            m0 = v0 - a * p1
+            m1 = v1 - a * p2
+            d0 = m0 + b_ * p0
+            d1 = m1 + b_ * p1
+            x[:, c] = x[:, c] + (a * p0 + a_ * d0)
+            f0 = m0 - a_ * d1
+            r0[:, c] = f0
             if not last:
-                images = n[:, c] + b * z[:, c]
-                watched = w[:, c] - a * images
-                s[:, c] = shadow
-                p[:, c] = direction
-                z[:, c] = images
-                w[:, c] = watched
-                keep_edges(c, watched)
-                rr = rr + residual * residual
-                rw = rw + residual * watched
-        return rr, rw, gamma, alpha
+                p3 = r3[:, c] + b * (inverse * (old2[:, c] - v2))
+                m2 = v2 - a * p3
+                d2 = m2 + b_ * p2
+                f1 = m1 - a_ * d2
+                r1[:, c] = f1
+                q0[:, c] = d0
+                q1[:, c] = d1
+                q2[:, c] = d2
+                old2[:, c] = m2
+                keep_edges(c, f1)
+                sums = added(
+                    sums,
+                    ((f0, f0), (f0, f1), (f1, f1), (f0, d1), (d0, d1), (f1, d1), (d1, d1), (f1, d2), (d1, d2)),
+                )
+        return sums, gamma, alpha_next
 
     unity = jnp.ones((1, 1), jnp.float32)
-    state = lax.fori_loop(0, ITERS - 1, iteration, (acc[0], acc[1], unity, unity))
-    iteration(ITERS - 1, state, last=True)
+    state = (opening[0] + (none,) * (DOTS - 4), unity, unity)
+    state = lax.fori_loop(0, ITERS // 2 - 1, block, state)
+    block(ITERS // 2 - 1, state, last=True)
 
 
 def solution(mesh):
@@ -308,11 +353,11 @@
             out_shape=(block, block),
             in_specs=[pl.BlockSpec(memory_space=pltpu.VMEM)] * 5,
             out_specs=[pl.BlockSpec(memory_space=pltpu.VMEM)] * 2,
-            scratch_shapes=[held(rows, cols)] * 8
+            scratch_shapes=[held(rows, cols)] * 10
             + [held(rows, LANES), held(1, cols), held(rows, LANES), held(1, cols)]
             + [held(2, rows, LANES), held(2, rows, LANES), held(2, 1, cols), held(2, 1, cols)]
             + [held(rows, LANES), held(rows, LANES), held(1, cols), held(1, cols)]
-            + [held(2, nc, 2, LANES), held(2, nr, 2, LANES)]
+            + [held(2, nc, DOTS, LANES), held(2, nr, 1, LANES)]
             + [dma((2,)), dma((2,)), dma((4,)), dma((2, 4)), dma((nc,)), dma((2, nc)), dma((nr,)), dma((2, nr))],
             compiler_params=pltpu.CompilerParams(collective_id=0, has_side_effects=True),
         )(*inputs)

time: 96.4 us -> 80.9 us (0.84)
  Pallas kernels: 93.2 us -> 77.7 us
    pallas_call x1, Pallas kernels: 93.2 us -> 77.7 us  [on_device(): pl.pallas_call(functools.partial(kernel, nr, nc), out_shape=(block, block...]
where the time goes in v2:
time: 80.9 us; the launch traced here: 80.8 us
  Pallas kernels  77.7 us (96%)
  local copies, waits for them, and re-layouts  2.42 us (3%)
    pallas_call x1, Pallas kernels, on_device(): pl.pallas_call(functools.partial(kernel, nr, nc), out_shape=(block, block...  77.7 us
    unnamed x4, local copies, waits for them, and re-layouts  2.42 us

profile of v2, /device:TPU:0, one launch (start us, length us, event | category | flops | bytes accessed | tf_op | source)
XLA Modules:
  0.0 80.8 jit_solution(10925295129583054336)
XLA Ops:
  0.6 77.7 %shard_map.68 = (f32[16,4096]{1,0:T(8,128)}, f32[16,4096]{1,0:T(8,128)}) custom-call(f32[16,4096]{1,0:T(8,128)} %depth.1, s32[16,4096]{1,0:T(8,128)} %hit_mask.1, s32[16,4096]{1,0:T(8,128)} %hit_count.1, f32[16,4096]{1,0:T(8,128)} %grad_h.1, f32[16,4096]{1,0:T(8,128)} %grad_v.1), custom_call_target="tpu_custom_call" | custom-call | tf_op jit(solution)/shard_map/pallas_call | solution.py:351
  78.3 0.0 copy-start
  78.3 1.7 %copy.9 = f32[16,4096]{1,0:T(8,128)} copy(f32[16,4096]{1,0:T(8,128)} %get-tuple-element.4) | data formatting | bytes 524288
  80.1 0.0 copy-done
  80.1 0.7 copy.10
Async XLA Ops:
  78.3 1.7 %copy-start = (f32[16,4096]{1,0:T(8,128)S(1)}, f32[16,4096]{1,0:T(8,128)}, u32[]{:S(2)}) copy-start(f32[16,4096]{1,0:T(8,128)} %get-tuple-element.5) | copy-start | bytes 786436

commit v3 on v2

--- a/solution.py
+++ b/solution.py
@@ -17,7 +17,7 @@
 
 
 def each(start, stop, body):
-    if stop - start <= 8:
+    if stop - start < 32:
         for k in range(start, stop):
             body(k)
     else:
@@ -31,8 +31,8 @@
     conf, east, south, r1, r2, r3, q0, q1, q2, old2,
     e_left, s_above, e_send, s_send,
     left, right, above, below, first_tile, last_tile, top, bottom,
-    by_col, by_row,
-    coef_send, coef_recv, halo_send, halo_recv, col_send, col_recv, row_send, row_recv,
+    folds, by_device,
+    coef_send, coef_recv, halo_send, halo_recv, sum_send, sum_recv,
 ):
     me_r = lax.axis_index("rows")
     me_c = lax.axis_index("cols")
@@ -41,15 +41,15 @@
     has_above, has_below = me_r > 0, me_r < nr - 1
     has_left, has_right = me_c > 0, me_c < nc - 1
 
-    def row_peer(k):
-        return (lax.rem(me_r + k, nr), me_c)
-
-    def col_peer(k):
-        return (me_r, lax.rem(me_c + k, nc))
+    devices = nr * nc
+    me = me_r * nc + me_c
+
+    def peer(k):
+        other = lax.rem(me + k, devices)
+        return (other // nc, lax.rem(other, nc))
 
     barrier = pltpu.get_barrier_semaphore()
-    each(1, nr, lambda k: pl.semaphore_signal(barrier, inc=1, device_id=row_peer(k), device_id_type=MESH))
-    each(1, nc, lambda k: pl.semaphore_signal(barrier, inc=1, device_id=col_peer(k), device_id_type=MESH))
+    each(1, devices, lambda k: pl.semaphore_signal(barrier, inc=1, device_id=peer(k), device_id_type=MESH))
 
     row_id = lax.broadcasted_iota(jnp.int32, (rows, LANES), 0)
     lane_id = lax.broadcasted_iota(jnp.int32, (rows, LANES), 1)
@@ -101,7 +101,7 @@
     def _():
         right[...] = jnp.zeros_like(right)
 
-    pl.semaphore_wait(barrier, nr - 1 + nc - 1)
+    pl.semaphore_wait(barrier, devices - 1)
 
     up, down = (me_r - 1, me_c), (me_r + 1, me_c)
     lefthand, righthand = (me_r, me_c - 1), (me_r, me_c + 1)
@@ -177,54 +177,34 @@
         if c.stop == cols:
             last_tile[...] = value
 
-    def reduce_cols(slot, sums):
+    def reduce(slot, sums):
         for k in range(DOTS):
-            by_col[slot, me_c, k : k + 1, :] = folded(sums[k])
-
-        def copy(k, source):
-            return remote(by_col.at[slot, me_c], by_col.at[slot, me_c], col_send.at[k], col_recv.at[slot, source], col_peer(k))
-
-        each(1, nc, lambda k: copy(k, me_c).start())
+            folds[k : k + 1, :] = folded(sums[k])
+        part = jnp.broadcast_to(jnp.sum(folds[...], axis=1, keepdims=True), (DOTS, LANES))
+        mine = lax.broadcasted_iota(jnp.int32, (DOTS, LANES), 0) == lax.broadcasted_iota(jnp.int32, (DOTS, LANES), 1)
+        by_device[slot, me] = folded(jnp.where(mine, part, 0.0))
+
+        def copy(k):
+            here = by_device.at[slot, me]
+            return remote(here, here, sum_send.at[k], sum_recv.at[slot, me], peer(k))
+
+        each(1, devices, lambda k: copy(k).start())
 
         def finish():
             def arrival(k):
-                source = lax.rem(me_c + k, nc)
-                here = by_col.at[slot, source]
-                remote(here, here, col_send.at[k], col_recv.at[slot, source], col_peer(k)).wait_recv()
-
-            each(1, nc, arrival)
-            each(1, nc, lambda k: copy(k, me_c).wait_send())
-            total = by_col[slot, 0]
-            for k in range(1, nc):
-                total = total + by_col[slot, k]
-            return total
-
-        return finish
-
-    def reduce_rows(slot, part):
-        part = jnp.broadcast_to(jnp.sum(part, axis=1, keepdims=True), (DOTS, LANES))
-        mine = lax.broadcasted_iota(jnp.int32, (DOTS, LANES), 0) == lax.broadcasted_iota(jnp.int32, (DOTS, LANES), 1)
-        by_row[slot, me_r] = folded(jnp.where(mine, part, 0.0))
-
-        def copy(k):
-            return remote(by_row.at[slot, me_r], by_row.at[slot, me_r], row_send.at[k], row_recv.at[slot, me_r], row_peer(k))
-
-        each(1, nr, lambda k: copy(k).start())
-
-        def finish():
-            def arrival(k):
-                source = lax.rem(me_r + k, nr)
-                here = by_row.at[slot, source]
-                remote(here, here, row_send.at[k], row_recv.at[slot, source], row_peer(k)).wait_recv()
-
-            each(1, nr, arrival)
-            each(1, nr, lambda k: copy(k).wait_send())
-            if nr <= 8:
-                total = by_row[slot, 0]
-                for k in range(1, nr):
-                    total = total + by_row[slot, k]
+                source = lax.rem(me + k, devices)
+                here = by_device.at[slot, source]
+                remote(here, here, sum_send.at[k], sum_recv.at[slot, source], peer(k)).wait_recv()
+
+            each(1, devices, arrival)
+            each(1, devices, lambda k: copy(k).wait_send())
+            if devices <= 32:
+                parts = [by_device[slot, k] for k in range(devices)]
+                while len(parts) > 1:
+                    parts = [a + b for a, b in zip(parts[::2], parts[1::2])] + parts[len(parts) // 2 * 2 :]
+                total = parts[0]
             else:
-                total = lax.fori_loop(1, nr, lambda k, t: t + by_row[slot, k], by_row[slot, 0])
+                total = lax.fori_loop(1, devices, lambda k, t: t + by_device[slot, k], by_device[slot, 0])
             return [total[:, k : k + 1] for k in range(DOTS)]
 
         return finish
@@ -281,11 +261,11 @@
         stencil(r1, 0, second)
         if not last:
             halos = exchange(1)
-        finish_rows = reduce_rows(slot, reduce_cols(slot, sums + cross[0])())
+        finish = reduce(slot, sums + cross[0])
         if not last:
             arrive(halos)
             stencil(r2, 1, stencil_into(r3, False))
-        r0r0, r0r1, r1r1, r0q1, q0q1, r1q1, q1q1, r1q2, q1q2, r1r2 = finish_rows()
+        r0r0, r0r1, r1r1, r0q1, q0q1, r1q1, q1q1, r1q2, q1q2, r1r2 = finish()
         beta = jnp.where(i == 0, jnp.zeros_like(r0r0), r0r0 / gamma_old)
         pap = r0r1 + beta * (2.0 * r0q1 + beta * q0q1)
         r0p1 = r0r1 + beta * r0q1
@@ -357,8 +337,8 @@
             + [held(rows, LANES), held(1, cols), held(rows, LANES), held(1, cols)]
             + [held(2, rows, LANES), held(2, rows, LANES), held(2, 1, cols), held(2, 1, cols)]
             + [held(rows, LANES), held(rows, LANES), held(1, cols), held(1, cols)]
-            + [held(2, nc, DOTS, LANES), held(2, nr, 1, LANES)]
-            + [dma((2,)), dma((2,)), dma((4,)), dma((2, 4)), dma((nc,)), dma((2, nc)), dma((nr,)), dma((2, nr))],
+            + [held(DOTS, LANES), held(2, nr * nc, 1, LANES)]
+            + [dma((2,)), dma((2,)), dma((4,)), dma((2, 4)), dma((nr * nc,)), dma((2, nr * nc))],
             compiler_params=pltpu.CompilerParams(collective_id=0, has_side_effects=True),
         )(*inputs)
 

time: 80.9 us -> 70.3 us (0.87)
  Pallas kernels: 77.7 us -> 67.1 us
    pallas_call x1, Pallas kernels: 77.7 us -> 67.1 us  [on_device(): pl.pallas_call(functools.partial(kernel, nr, nc), out_shape=(block, block...]
where the time goes in v3:
time: 70.3 us; the launch traced here: 70.1 us
  Pallas kernels  67.1 us (95%)
  local copies, waits for them, and re-layouts  2.42 us (3%)
    pallas_call x1, Pallas kernels, on_device(): pl.pallas_call(functools.partial(kernel, nr, nc), out_shape=(block, block...  67.1 us
    unnamed x4, local copies, waits for them, and re-layouts  2.42 us

profile of v3, /device:TPU:0, one launch (start us, length us, event | category | flops | bytes accessed | tf_op | source)
XLA Modules:
  0.0 70.1 jit_solution(11632607621334136806)
XLA Ops:
  0.6 67.1 %shard_map.68 = (f32[16,4096]{1,0:T(8,128)}, f32[16,4096]{1,0:T(8,128)}) custom-call(f32[16,4096]{1,0:T(8,128)} %depth.1, s32[16,4096]{1,0:T(8,128)} %hit_mask.1, s32[16,4096]{1,0:T(8,128)} %hit_count.1, f32[16,4096]{1,0:T(8,128)} %grad_h.1, f32[16,4096]{1,0:T(8,128)} %grad_v.1), custom_call_target="tpu_custom_call" | custom-call | tf_op jit(solution)/shard_map/pallas_call | solution.py:331
  67.7 0.0 copy-start
  67.7 1.7 %copy.9 = f32[16,4096]{1,0:T(8,128)} copy(f32[16,4096]{1,0:T(8,128)} %get-tuple-element.4) | data formatting | bytes 524288
  69.4 0.0 copy-done
  69.4 0.7 %copy.10 = f32[16,4096]{1,0:T(8,128)} copy(f32[16,4096]{1,0:T(8,128)S(1)} %copy-done) | data formatting | bytes 524288
Async XLA Ops:
  67.7 1.7 %copy-start = (f32[16,4096]{1,0:T(8,128)S(1)}, f32[16,4096]{1,0:T(8,128)}, u32[]{:S(2)}) copy-start(f32[16,4096]{1,0:T(8,128)} %get-tuple-element.5) | copy-start | bytes 786436

commit v4 on v3

--- a/solution.py
+++ b/solution.py
@@ -137,31 +137,55 @@
         for copy, sends, _ in copies:
             pl.when(sends)(copy.wait_send)
 
-    def stencil(src, slot, emit):
-        def to_left(v):
-            return pltpu.roll(v, LANES - 1, 1)
-
-        def to_right(v):
-            return pltpu.roll(v, 1, 1)
-
+    def to_left(v):
+        return pltpu.roll(v, LANES - 1, 1)
+
+    def to_right(v):
+        return pltpu.roll(v, 1, 1)
+
+    def stencil(src, dst):
         v = src[:, at(0)]
-        moved = to_left(v)
-        before = left[slot]
-        flow = e_left[...] * (before - jnp.where(lane_id < LANES - 1, to_left(before), moved))
-        carried = to_right(flow)
+        moved, carried = to_left(v), jnp.zeros((rows, LANES), jnp.float32)
         for j in range(tiles):
             c = at(j)
-            following = src[:, at(j + 1)] if j + 1 < tiles else right[slot]
-            moved_next = to_left(following)
+            final = j + 1 == tiles
+            following = v if final else src[:, at(j + 1)]
+            moved_next = v if final else to_left(following)
             flow = east[:, c] * (v - jnp.where(lane_id < LANES - 1, moved, moved_next))
+            if final:
+                flow = jnp.where(lane_id < LANES - 1, flow, 0.0)
             shifted = to_right(flow)
             from_left = jnp.where(lane_id > 0, shifted, carried)
-            lower = jnp.where(row_id < rows - 1, pltpu.roll(v, rows - 1, 0), below[slot, :, c])
-            fall = south[:, c] * (v - lower)
-            upper = s_above[:, c] * (above[slot, :, c] - v)
-            from_above = jnp.where(row_id > 0, pltpu.roll(fall, 1, 0), upper)
-            emit(c, v, conf[:, c] * v + ((flow - from_left) + (fall - from_above)))
+            fall = jnp.where(row_id < rows - 1, south[:, c] * (v - pltpu.roll(v, rows - 1, 0)), 0.0)
+            dst[:, c] = conf[:, c] * v + ((flow - from_left) + (fall - pltpu.roll(fall, 1, 0)))
             v, moved, carried = following, moved_next, shifted
+
+    def finish_edges(src, dst, slot):
+        v = src[:, at(0)]
+        near = to_left(v)
+        flow = to_right(e_left[...] * (left[slot] - near))
+        dst[:, at(0)] = dst[:, at(0)] - jnp.where(lane_id == 0, flow, 0.0)
+        c = at(tiles - 1)
+        v = src[:, c]
+        flow = east[:, c] * (v - to_left(right[slot]))
+        dst[:, c] = dst[:, c] + jnp.where(lane_id == LANES - 1, flow, 0.0)
+        upper = s_above[...] * (above[slot] - src[0:1, :])
+        dst[0:1, :] = dst[0:1, :] - upper
+        lower = south[rows - 1 :, :] * (src[rows - 1 :, :] - below[slot])
+        dst[rows - 1 :, :] = dst[rows - 1 :, :] + lower
+
+    def keep_all_edges(value):
+        top[...] = value[:1, :]
+        bottom[...] = value[rows - 1 :, :]
+        first_tile[...] = value[:, at(0)]
+        last_tile[...] = value[:, at(tiles - 1)]
+
+    def dots(pairs):
+        sums = [jnp.zeros((rows, LANES), jnp.float32)] * len(pairs)
+        for j in range(tiles):
+            c = at(j)
+            sums = [total + a[:, c] * b[:, c] for total, (a, b) in zip(sums, pairs)]
+        return tuple(sums)
 
     def folded(acc):
         return jnp.sum(acc, axis=0, keepdims=True)
@@ -215,14 +239,6 @@
     def added(sums, pairs):
         return tuple(total + a * b for total, (a, b) in zip(sums, pairs))
 
-    def stencil_into(dst, edges):
-        def emit(c, v, image):
-            dst[:, c] = image
-            if edges:
-                keep_edges(c, image)
-
-        return emit
-
     def exchange(slot):
         halos = halo_copies(slot)
         start(halos)
@@ -234,37 +250,29 @@
 
     first, coefs = exchange(1), coef_copies()
     start(coefs)
+    stencil(r0, r1)
     arrive(first)
     arrive(coefs)
+    finish_edges(r0, r1, 1)
+    keep_all_edges(r1)
     none = jnp.zeros((rows, LANES), jnp.float32)
-    opening = [(none,) * 3]
-
-    def begin(c, v, image):
-        r1[:, c] = image
-        keep_edges(c, image)
-        opening[0] = added(opening[0], ((v, v), (v, image), (image, image)))
-
-    stencil(r0, 1, begin)
+    opening = dots(((r0, r0), (r0, r1), (r1, r1)))
 
     def block(i, state, last=False):
         sums, gamma_old, alpha_old = state
         slot = lax.rem(i, 2)
-        arrive(exchange(0))
-        cross = [(none,)]
-
-        def second(c, v, image):
-            r2[:, c] = image
-            if not last:
-                keep_edges(c, image)
-            cross[0] = added(cross[0], ((v, image),))
-
-        stencil(r1, 0, second)
+        halos = exchange(0)
+        stencil(r1, r2)
+        arrive(halos)
+        finish_edges(r1, r2, 0)
         if not last:
+            keep_all_edges(r2)
             halos = exchange(1)
-        finish = reduce(slot, sums + cross[0])
+        finish = reduce(slot, sums + dots(((r1, r2),)))
         if not last:
+            stencil(r2, r3)
             arrive(halos)
-            stencil(r2, 1, stencil_into(r3, False))
+            finish_edges(r2, r3, 1)
         r0r0, r0r1, r1r1, r0q1, q0q1, r1q1, q1q1, r1q2, q1q2, r1r2 = finish()
         beta = jnp.where(i == 0, jnp.zeros_like(r0r0), r0r0 / gamma_old)
         pap = r0r1 + beta * (2.0 * r0q1 + beta * q0q1)
@@ -312,7 +320,7 @@
         return sums, gamma, alpha_next
 
     unity = jnp.ones((1, 1), jnp.float32)
-    state = (opening[0] + (none,) * (DOTS - 4), unity, unity)
+    state = (opening + (none,) * (DOTS - 4), unity, unity)
     state = lax.fori_loop(0, ITERS // 2 - 1, block, state)
     block(ITERS // 2 - 1, state, last=True)
 

time: 70.3 us -> 69.6 us (0.990)
    pallas_call x1, Pallas kernels: 67.1 us -> 66.4 us  [on_device(): pl.pallas_call(functools.partial(kernel, nr, nc), out_shape=(block, block...]
where the time goes in v4:
time: 69.6 us; the launch traced here: 69.4 us
  Pallas kernels  66.4 us (95%)
  local copies, waits for them, and re-layouts  2.42 us (3%)
    pallas_call x1, Pallas kernels, on_device(): pl.pallas_call(functools.partial(kernel, nr, nc), out_shape=(block, block...  66.4 us
    unnamed x4, local copies, waits for them, and re-layouts  2.42 us

profile of v4, /device:TPU:0, one launch (start us, length us, event | category | flops | bytes accessed | tf_op | source)
XLA Modules:
  0.0 69.4 jit_solution(4646057132387045354)
XLA Ops:
  0.6 66.4 %shard_map.68 = (f32[16,4096]{1,0:T(8,128)}, f32[16,4096]{1,0:T(8,128)}) custom-call(f32[16,4096]{1,0:T(8,128)} %depth.1, s32[16,4096]{1,0:T(8,128)} %hit_mask.1, s32[16,4096]{1,0:T(8,128)} %hit_count.1, f32[16,4096]{1,0:T(8,128)} %grad_h.1, f32[16,4096]{1,0:T(8,128)} %grad_v.1), custom_call_target="tpu_custom_call" | custom-call | tf_op jit(solution)/shard_map/pallas_call | solution.py:339
  67.0 0.0 copy-start
  67.0 1.7 %copy.9 = f32[16,4096]{1,0:T(8,128)} copy(f32[16,4096]{1,0:T(8,128)} %get-tuple-element.4) | data formatting | bytes 524288
  68.7 0.0 copy-done
  68.7 0.7 %copy.10 = f32[16,4096]{1,0:T(8,128)} copy(f32[16,4096]{1,0:T(8,128)S(1)} %copy-done) | data formatting | bytes 524288
Async XLA Ops:
  67.0 1.7 %copy-start = (f32[16,4096]{1,0:T(8,128)S(1)}, f32[16,4096]{1,0:T(8,128)}, u32[]{:S(2)}) copy-start(f32[16,4096]{1,0:T(8,128)} %get-tuple-element.5) | copy-start | bytes 786436
